TPU v7x, 32 devices: a whole 2x2x4 slice. The times are simulated.
32 devices in a mesh: chan: 16 (over z, x, core), tm: 2 (over y).
Axes of the slice: x: 2, y: 2, z: 4, core: 2. Of those that a mesh axis runs over, the one named last changes fastest.
Arguments:
- volt: bfloat16 [2, 64, 2048, 512], P(None, None, ('chan', 'tm')), may hold values from -40 to 40
- windows: int32 [64, 2], P('chan'), may hold values from 0 to 2048, as said below
- start_basis: float32 [2, 64, 8, 512], P(None, 'chan'), may hold values from -6 to 6
- positions: float32 [2, 512], replicated, may hold values from -16 to 16
- pointing: float32 [2, 1024], replicated, may hold values from -0.7 to 0.7
- beam_dir: int32 [1024], replicated, may hold values from 0 to 1023, each once
Outputs:
- power: float32 [64, 1024], P('chan', 'tm')
Inputs may be any that keep to these rules, and one draw needn't show every extreme that they name: `windows`: each row holds a channel's first window sample and one past its last; every window holds 1024 samples or more. `beam_dir`: each table entry is named by exactly one beam.
All inputs are finite; a program needn't handle non-finite values.
Results may differ from a plain program's by a relative error of at most 0.0024.
Values may be sent and summed in bfloat16 or wider, within the bound.
No kernel may reach another device: no remote copies, remote signals or barrier semaphores. Data moves between devices by JAX's collectives and lax.ppermute only.
A program may use at most 128 MiB of HBM per device.

v0:
```python
import math
import jax
import jax.numpy as jnp
from jax import lax
from jax.sharding import PartitionSpec as P

ITERS = 6
EPS = 1e-06
TWO_PI = 2.0 * math.pi


def orthonormal(real_part, imag_part):
    number = real_part.shape[-2]
    base_real = []
    base_imag = []
    for column in range(number):
        vec_real = real_part[..., column, :]
        vec_imag = imag_part[..., column, :]
        for earlier in range(column):
            prev_real = base_real[earlier]
            prev_imag = base_imag[earlier]
            coef_real = jnp.sum(prev_real * vec_real + prev_imag * vec_imag, axis=-1, keepdims=True)
            coef_imag = jnp.sum(prev_real * vec_imag - prev_imag * vec_real, axis=-1, keepdims=True)
            vec_real = vec_real - (coef_real * prev_real - coef_imag * prev_imag)
            vec_imag = vec_imag - (coef_real * prev_imag + coef_imag * prev_real)
        inverse = lax.rsqrt(
            jnp.sum(vec_real * vec_real + vec_imag * vec_imag, axis=-1, keepdims=True) + EPS
        )
        base_real.append(vec_real * inverse)
        base_imag.append(vec_imag * inverse)
    return (jnp.stack(base_real, axis=-2), jnp.stack(base_imag, axis=-2))


def fdot(left, right):
    return jnp.dot(left, right, preferred_element_type=jnp.float32)


def fsum(form, left, right):
    return jnp.einsum(form, left, right, preferred_element_type=jnp.float32)


def channel_power(volt_real, volt_imag, base_real, base_imag, freq, direction, positions):
    low_real = base_real.astype(jnp.bfloat16)
    low_imag = base_imag.astype(jnp.bfloat16)
    full_real = (fdot(volt_real, low_real.T) + fdot(volt_imag, low_imag.T)).astype(jnp.bfloat16)
    full_imag = (fdot(volt_imag, low_real.T) - fdot(volt_real, low_imag.T)).astype(jnp.bfloat16)
    removed_real = fdot(full_real, low_real) - fdot(full_imag, low_imag)
    removed_imag = fdot(full_real, low_imag) + fdot(full_imag, low_real)
    clean_real = (volt_real.astype(jnp.float32) - removed_real).astype(jnp.bfloat16)
    clean_imag = (volt_imag.astype(jnp.float32) - removed_imag).astype(jnp.bfloat16)
    phase = (
        TWO_PI
        * freq
        * (
            positions[0][:, None] * direction[0][None, :]
            + positions[1][:, None] * direction[1][None, :]
        )
    )
    steer_real = jnp.cos(phase).astype(jnp.bfloat16)
    steer_imag = jnp.sin(phase).astype(jnp.bfloat16)
    beam_real = fdot(clean_real, steer_real) + fdot(clean_imag, steer_imag)
    beam_imag = fdot(clean_imag, steer_real) - fdot(clean_real, steer_imag)
    return jnp.sum(beam_real * beam_real + beam_imag * beam_imag, axis=0)


def body(volt, windows, start_basis, positions, pointing, beam_dir):
    parts, channels_all, rows_in, stations = volt.shape
    n_chan = lax.axis_size("chan")
    n_time = lax.axis_size("tm")
    chan_dev = channels_all // n_chan
    chan_at = lax.axis_index("chan")
    time_at = lax.axis_index("tm")
    total_time = rows_in * n_chan * n_time
    per_device = chan_dev // n_time
    blocks = volt.reshape(parts, n_chan * n_time, per_device, rows_in, stations)
    moved = lax.all_to_all(blocks, ("chan", "tm"), split_axis=1, concat_axis=3, tiled=True)
    local = moved.reshape(parts, per_device, total_time, stations)
    sample_at = jnp.arange(total_time, dtype=jnp.int32)
    first_channel = chan_at * chan_dev + time_at * per_device
    own_windows = lax.dynamic_slice_in_dim(windows, time_at * per_device, per_device, 0)
    own_basis = lax.dynamic_slice_in_dim(start_basis, time_at * per_device, per_device, 1)
    volt_real = local[0]
    volt_imag = local[1]
    window_mask = (
        (sample_at[None, :] >= own_windows[:, 0:1]) & (sample_at[None, :] < own_windows[:, 1:2])
    ).astype(jnp.float32)
    base_real, base_imag = orthonormal(own_basis[0], own_basis[1])
    for iteration in range(ITERS):
        low_real = base_real.astype(jnp.bfloat16)
        low_imag = base_imag.astype(jnp.bfloat16)
        proj_real = fsum("cts,cks->ctk", volt_real, low_real) + fsum(
            "cts,cks->ctk", volt_imag, low_imag
        )
        proj_imag = fsum("cts,cks->ctk", volt_imag, low_real) - fsum(
            "cts,cks->ctk", volt_real, low_imag
        )
        proj_real = (proj_real * window_mask[:, :, None]).astype(jnp.bfloat16)
        proj_imag = (proj_imag * window_mask[:, :, None]).astype(jnp.bfloat16)
        image_real = fsum("ctk,cts->cks", proj_real, volt_real) - fsum(
            "ctk,cts->cks", proj_imag, volt_imag
        )
        image_imag = fsum("ctk,cts->cks", proj_real, volt_imag) + fsum(
            "ctk,cts->cks", proj_imag, volt_real
        )
        base_real, base_imag = orthonormal(image_real, image_imag)
    direction = jnp.take(pointing, beam_dir, axis=1)
    channel_ids = first_channel + jnp.arange(volt_real.shape[0], dtype=jnp.int32)

    def one_channel(inputs):
        chan_real, chan_imag, basis_re, basis_im, channel = inputs
        freq = 1.0 + channel.astype(jnp.float32) / channels_all
        return channel_power(chan_real, chan_imag, basis_re, basis_im, freq, direction, positions)

    partial_power = lax.map(one_channel, (volt_real, volt_imag, base_real, base_imag, channel_ids))
    scaled = partial_power / (total_time * stations)
    return lax.all_to_all(scaled, "tm", split_axis=1, concat_axis=0, tiled=True)


def solution(mesh):
    return jax.shard_map(
        body,
        mesh=mesh,
        in_specs=(
            P(None, None, ("chan", "tm"), None),
            P("chan", None),
            P(None, "chan", None, None),
            P(),
            P(),
            P(),
        ),
        out_specs=P("chan", "tm"),
        check_vma=False,
    )
```

profile of v0, /device:TPU:2, one launch (start us, length us, event | category | flops | bytes accessed | tf_op | source)
XLA Modules:
  0.0 407.5 jit_solution(8869985679007207590)
XLA Ops:
  0.0 7.7 %copy.2137 = bf16[2,32,2,64,512]{4,3,2,0,1:T(8,128)(2,1)} copy(bf16[2,32,2,64,512]{4,3,2,1,0:T(8,128)(2,1)} %bitcast.1410) | data formatting | bytes 16777216 | tf_op jit(solution)/shard_map/reshape | solution.py:75
  7.7 6.2 %all-to-all-start = ((bf16[2,32,2,64,512]{4,3,2,0,1:T(8,128)(2,1)}), bf16[2,32,2,64,512]{4,3,2,0,1:T(8,128)(2,1)}, u32[]{:S(2)}, u32[]{:S(2)}) async-start(bf16[2,32,2,64,512]{4,3,2,0,1:T(8,128)(2,1)} %copy.2137), calls=%async_computation | async-start | bytes 16777216 | tf_op jit(solution)/shard_map/all_to_all | solution.py:76
  14.2 2.8 gather_fusion
  22.7 175.2 %all-to-all-done = bf16[2,32,2,64,512]{4,3,2,0,1:T(8,128)(2,1)} async-done(((bf16[2,32,2,64,512]{4,3,2,0,1:T(8,128)(2,1)}), bf16[2,32,2,64,512]{4,3,2,0,1:T(8,128)(2,1)}, u32[]{:S(2)}, u32[]{:S(2)}) %all-to-all-start) | async-done | bytes 8388640 | tf_op jit(solution)/shard_map/all_to_all | solution.py:76
  197.9 4.2 %fusion.294 = (bf16[1,1,2,32,64,512]{5,4,2,0,3,1:T(8,128)(2,1)S(1)}, bf16[1,1,2,32,64,512]{5,4,2,0,3,1:T(8,128)(2,1)S(1)}) fusion(bf16[2,1,2,32,64,512]{5,4,2,0,3,1:T(8,128)(2,1)} %bitcast.12), kind=kLoop, calls=%fused_computation.1637 | loop fusion | bytes 16777216 | tf_op jit(solution)/shard_map/slice | solution.py:83
  216.8 1.2 fusion.36
  228.2 1.6 fusion.65
  254.8 1.4 fusion.42
  278.8 117.9 %while.10 = (s32[]{:T(128)}, f32[2,1024]{1,0:T(2,128)S(1)}, bf16[2,2048,512]{2,1,0:T(8,128)(2,1)}, bf16[2,8,512]{2,0,1:T(2,128)(2,1)S(1)}, bf16[2,2048,512]{2,1,...) while((s32[]{:T(128)}, f32[2,1024]{1,0:T(2,128)S(1)}, ...), condition=%wide.region_450.451_spmd, body=%wide.region_448.0_spmd.sunk | while | flops 8755674112 | bytes 126480664 | solution.py:114
  302.9 2.2 fusion.463
  305.1 2.2 fusion.464
  307.4 2.4 fusion.460
  313.5 8.5 %fusion.470 = f32[2048,1024]{1,0:T(8,128)S(1)} fusion(bf16[2048,512]{1,0:T(8,128)(2,1)S(1)} %subtract_convert_fusion.4, f32[1024]{0:T(1024)S(1)} %bitcast.1416, f32[512]{0:T(512)S(1)} %bitcast.1424, f32[1024]{0:T(1024)S(1)} %bitcast.1412, f32[512]{0:T(512)S(1)} %bitcast.1420, f32[]{:T(128)} %bitcast.1358), kind=kOutput, calls=%fused_computation.23.clone.1 | convolution fusion | flops 2150105088 | bytes 10498052 | tf_op jit(solution)/shard_map/while/body/eval_jaxpr/dot_general | solution.py:35
  321.9 8.4 %fusion.467 = f32[2048,1024]{1,0:T(8,128)S(1)} fusion(bf16[2048,512]{1,0:T(8,128)(2,1)S(1)} %subtract_convert_fusion.4, f32[1024]{0:T(1024)S(1)} %bitcast.1417, f32[512]{0:T(512)S(1)} %bitcast.1425, f32[1024]{0:T(1024)S(1)} %bitcast.1413, f32[512]{0:T(512)S(1)} %bitcast.1421, f32[]{:T(128)} %bitcast.1358), kind=kOutput, calls=%fused_computation.21.clone.1 | convolution fusion | flops 2150105088 | bytes 10498052 | tf_op jit(solution)/shard_map/while/body/eval_jaxpr/dot_general | solution.py:35
  330.3 8.4 %fusion.469 = f32[2048,1024]{1,0:T(8,128)S(1)} fusion(bf16[2048,512]{1,0:T(8,128)(2,1)S(1)} %subtract_convert_fusion.5, f32[1024]{0:T(1024)S(1)} %bitcast.1418, f32[512]{0:T(512)S(1)} %bitcast.1426, f32[1024]{0:T(1024)S(1)} %bitcast.1414, f32[512]{0:T(512)S(1)} %bitcast.1422, f32[]{:T(128)} %bitcast.1358), kind=kOutput, calls=%fused_computation.22.clone.1 | convolution fusion | flops 2150105088 | bytes 10498052 | tf_op jit(solution)/shard_map/while/body/eval_jaxpr/dot_general | solution.py:35
  338.8 10.2 %add_reduce_fusion.198 = f32[1024]{0:T(1024)S(1)} fusion(f32[2048,1024]{1,0:T(8,128)S(1)} %fusion.467, f32[2048,1024]{1,0:T(8,128)S(1)} %fusion.469, f32[2048,1024]{1,0:T(8,128)S(1)} %fusion.470, bf16[2048,512]{1,0:T(8,128)(2,1)S(1)} %subtract_convert_fusion.5, f32[1024]{0:T(1024)S(1)} %bitcast.1419, f32[512]{0:T(512)S(1)} %bitcast.1427, ...), kind=kOutput, calls=%fused_computation.1.clone.1 | convolution fusion | flops 2162686976 | bytes 27279364 | tf_op jit(solution)/shard_map/while/body/eval_jaxpr/dot_general | solution.py:35
  350.6 2.2 fusion.463
  352.8 2.2 fusion.464
  355.1 2.4 fusion.460
  361.2 8.5 %fusion.470 = f32[2048,1024]{1,0:T(8,128)S(1)} fusion(bf16[2048,512]{1,0:T(8,128)(2,1)S(1)} %subtract_convert_fusion.4, f32[1024]{0:T(1024)S(1)} %bitcast.1416, f32[512]{0:T(512)S(1)} %bitcast.1424, f32[1024]{0:T(1024)S(1)} %bitcast.1412, f32[512]{0:T(512)S(1)} %bitcast.1420, f32[]{:T(128)} %bitcast.1358), kind=kOutput, calls=%fused_computation.23.clone.1 | convolution fusion | flops 2150105088 | bytes 10498052 | tf_op jit(solution)/shard_map/while/body/eval_jaxpr/dot_general | solution.py:35
  369.6 8.4 %fusion.467 = f32[2048,1024]{1,0:T(8,128)S(1)} fusion(bf16[2048,512]{1,0:T(8,128)(2,1)S(1)} %subtract_convert_fusion.4, f32[1024]{0:T(1024)S(1)} %bitcast.1417, f32[512]{0:T(512)S(1)} %bitcast.1425, f32[1024]{0:T(1024)S(1)} %bitcast.1413, f32[512]{0:T(512)S(1)} %bitcast.1421, f32[]{:T(128)} %bitcast.1358), kind=kOutput, calls=%fused_computation.21.clone.1 | convolution fusion | flops 2150105088 | bytes 10498052 | tf_op jit(solution)/shard_map/while/body/eval_jaxpr/dot_general | solution.py:35
  378.0 8.4 %fusion.469 = f32[2048,1024]{1,0:T(8,128)S(1)} fusion(bf16[2048,512]{1,0:T(8,128)(2,1)S(1)} %subtract_convert_fusion.5, f32[1024]{0:T(1024)S(1)} %bitcast.1418, f32[512]{0:T(512)S(1)} %bitcast.1426, f32[1024]{0:T(1024)S(1)} %bitcast.1414, f32[512]{0:T(512)S(1)} %bitcast.1422, f32[]{:T(128)} %bitcast.1358), kind=kOutput, calls=%fused_computation.22.clone.1 | convolution fusion | flops 2150105088 | bytes 10498052 | tf_op jit(solution)/shard_map/while/body/eval_jaxpr/dot_general | solution.py:35
  386.5 10.2 %add_reduce_fusion.198 = f32[1024]{0:T(1024)S(1)} fusion(f32[2048,1024]{1,0:T(8,128)S(1)} %fusion.467, f32[2048,1024]{1,0:T(8,128)S(1)} %fusion.469, f32[2048,1024]{1,0:T(8,128)S(1)} %fusion.470, bf16[2048,512]{1,0:T(8,128)(2,1)S(1)} %subtract_convert_fusion.5, f32[1024]{0:T(1024)S(1)} %bitcast.1419, f32[512]{0:T(512)S(1)} %bitcast.1427, ...), kind=kOutput, calls=%fused_computation.1.clone.1 | convolution fusion | flops 2162686976 | bytes 27279364 | tf_op jit(solution)/shard_map/while/body/eval_jaxpr/dot_general | solution.py:35
  396.8 9.7 %all_to_all.34 = f32[2,2,512]{2,0,1:T(2,128)S(1)} all-to-all(f32[2,2,512]{2,0,1:T(2,128)S(1)} %bitcast.1428), channel_id=1, replica_groups=mesh['chan'=16,'tm'=2] {'tm'}, dimensions={1} | all-to-all | bytes 16384 | tf_op jit(solution)/shard_map/all_to_all | solution.py:116
  (390 shorter events, 87.2 us)
Async XLA Ops:
  0.0 17.4 %copy-start = (s32[4,2]{0,1:T(2,128)S(1)}, s32[4,2]{0,1:T(2,128)}, u32[]{:S(2)}) copy-start(s32[4,2]{0,1:T(2,128)} %param.9) | copy-start | bytes 100
  7.7 6.2 %copy-start.9 = (f32[2,1024]{1,0:T(2,128)S(1)}, f32[2,1024]{1,0:T(2,128)}, u32[]{:S(2)}) copy-start(f32[2,1024]{1,0:T(2,128)} %param.12) | copy-start | bytes 24580
  7.7 6.5 %copy-start.8 = (s32[1024]{0:T(1024)S(1)}, s32[1024]{0:T(1024)}, u32[]{:S(2)}) copy-start(s32[1024]{0:T(1024)} %param.13) | copy-start | bytes 12292
  7.7 9.8 %copy-start.7 = (f32[2,4,8,512]{3,2,1,0:T(8,128)S(1)}, f32[2,4,8,512]{3,2,1,0:T(8,128)}, u32[]{:S(2)}) copy-start(f32[2,4,8,512]{3,2,1,0:T(8,128)} %param.10) | copy-start | bytes 393220
  7.7 190.2 %all-to-all-start = ((bf16[2,32,2,64,512]{4,3,2,0,1:T(8,128)(2,1)}), bf16[2,32,2,64,512]{4,3,2,0,1:T(8,128)(2,1)}, u32[]{:S(2)}, u32[]{:S(2)}) async-start(bf16[2,32,2,64,512]{4,3,2,0,1:T(8,128)(2,1)} %copy.2137), calls=%async_computation | async-start | bytes 16777216 | tf_op jit(solution)/shard_map/all_to_all | solution.py:76
  202.6 69.8 %copy-start.2 = (bf16[1,1,2,32,64,512]{5,4,3,2,1,0:T(8,128)(2,1)}, bf16[1,1,2,32,64,512]{5,4,3,2,1,0:T(8,128)(2,1)S(1)}, u32[]{:S(2)}) copy-start(bf16[1,1,2,32,64,512]{5,4,3,2,1,0:T(8,128)(2,1)S(1)} %copy.2141) | copy-start | bytes 12582916
  203.1 70.0 %copy-start.4 = (bf16[1,1,2,32,64,512]{5,4,3,2,1,0:T(8,128)(2,1)}, bf16[1,1,2,32,64,512]{5,4,3,2,1,0:T(8,128)(2,1)S(1)}, u32[]{:S(2)}) copy-start(bf16[1,1,2,32,64,512]{5,4,3,2,1,0:T(8,128)(2,1)S(1)} %copy.2138) | copy-start | bytes 12582916
  272.4 6.4 %copy-start.6 = (f32[2,512]{1,0:T(2,128)S(1)}, f32[2,512]{1,0:T(2,128)}, u32[]{:S(2)}) copy-start(f32[2,512]{1,0:T(2,128)} %param.11) | copy-start | bytes 12292
  301.4 8.4 %copy-start.3 = (bf16[2,2048,512]{2,1,0:T(8,128)(2,1)S(1)}, bf16[2,2048,512]{2,1,0:T(8,128)(2,1)}, u32[]{:S(2)}) copy-start(bf16[2,2048,512]{2,1,0:T(8,128)(2,1)} %get-tuple-element.1442) | copy-start | bytes 12582916 | tf_op jit(solution)/shard_map/while
  307.4 3.8 copy-start.5
  349.1 8.4 %copy-start.3 = (bf16[2,2048,512]{2,1,0:T(8,128)(2,1)S(1)}, bf16[2,2048,512]{2,1,0:T(8,128)(2,1)}, u32[]{:S(2)}) copy-start(bf16[2,2048,512]{2,1,0:T(8,128)(2,1)} %get-tuple-element.1442) | copy-start | bytes 12582916 | tf_op jit(solution)/shard_map/while
  355.1 3.8 copy-start.5
  396.8 10.3 %copy-start.1 = (s32[4,2]{0,1:T(2,128)S(1)}, s32[4,2]{0,1:T(2,128)}, u32[]{:S(2)}) copy-start(s32[4,2]{0,1:T(2,128)} %param.9) | copy-start | bytes 100
where the time goes:
time: 411 us; the launch traced here: 407 us
  waiting for transfers between devices  175 us (43%)
  matrix products  137 us (33%)
  other arithmetic  35.5 us (9%)
  loops' own time  24.5 us (6%)
  local copies, waits for them, and re-layouts  18.3 us (4%)
  blocking collectives  9.7 us (2%)
  starting transfers between devices  6.18 us (2%)
    all_to_all x1, waiting for transfers between devices, body(): lax.all_to_all(blocks, ('chan', 'tm'), split_axis=1, concat_axis=3, tiled...  175 us
    dot_general x24, matrix products, fdot(): return jnp.dot(left, right, preferred_element_type=jnp.float32)  92.1 us
    dot_general x48, matrix products, fsum(): return jnp.einsum(form, left, right, preferred_element_type=jnp.float32)  44.9 us
    another operation x1, loops' own time, body(): lax.map(one_channel, (volt_real, volt_imag, base_real, base_imag, channel...  24.5 us
    reduce_sum x56, other arithmetic, orthonormal(): jnp.sum(prev_real * vec_real + prev_imag * vec_imag, axis=-1, keepdims=True)  16.2 us
    reduce_sum x56, other arithmetic, orthonormal(): jnp.sum(vec_real * vec_real + vec_imag * vec_imag, axis=-1, keepdims=True)  10.4 us
    all_to_all x1, blocking collectives, body(): return lax.all_to_all(scaled, 'tm', split_axis=1, concat_axis=0, tiled=True)  9.7 us
  transfers between devices with their start and end apart: 1, of which 1 were waited for; matrix products, arithmetic and copies ran while one was open for 2% of the time, Pallas kernels for 0%

commit v1 on v0

--- a/solution.py
+++ b/solution.py
@@ -73,7 +73,15 @@
     total_time = rows_in * n_chan * n_time
     per_device = chan_dev // n_time
     blocks = volt.reshape(parts, n_chan * n_time, per_device, rows_in, stations)
-    moved = lax.all_to_all(blocks, ("chan", "tm"), split_axis=1, concat_axis=3, tiled=True)
+    moved = jnp.concatenate(
+        lax.all_to_all(
+            jnp.stack(jnp.split(blocks, lax.axis_size(("chan", "tm")), axis=1)),
+            ("chan", "tm"),
+            0,
+            0,
+        ),
+        axis=3,
+    )
     local = moved.reshape(parts, per_device, total_time, stations)
     sample_at = jnp.arange(total_time, dtype=jnp.int32)
     first_channel = chan_at * chan_dev + time_at * per_device

time: 411 us -> 424 us (1.032)
  local copies, waits for them, and re-layouts: 18.3 us -> 30.3 us
    unnamed x23 -> x58, local copies, waits for them, and re-layouts: 0.33 us -> 20 us
    reshape x1 -> x0, local copies, waits for them, and re-layouts: 7.72 us -> none  [body(): blocks = volt.reshape(parts, n_chan * n_time, per_device, rows_in, stations)]
where the time goes in v1:
time: 424 us; the launch traced here: 420 us
  waiting for transfers between devices  175 us (41%)
  matrix products  137 us (32%)
  other arithmetic  35.5 us (8%)
  local copies, waits for them, and re-layouts  30.3 us (7%)
  loops' own time  24.5 us (6%)
  blocking collectives  9.72 us (2%)
  starting transfers between devices  6.18 us (1%)
    all_to_all x1, waiting for transfers between devices, body(): lax.all_to_all(jnp.stack(jnp.split(blocks, lax.axis_size(('chan', 'tm')),...  175 us
    dot_general x24, matrix products, fdot(): return jnp.dot(left, right, preferred_element_type=jnp.float32)  92.3 us
    dot_general x48, matrix products, fsum(): return jnp.einsum(form, left, right, preferred_element_type=jnp.float32)  44.9 us
    another operation x1, loops' own time, body(): lax.map(one_channel, (volt_real, volt_imag, base_real, base_imag, channel...  24.5 us
    unnamed x58, local copies, waits for them, and re-layouts  20 us
    reduce_sum x56, other arithmetic, orthonormal(): jnp.sum(prev_real * vec_real + prev_imag * vec_imag, axis=-1, keepdims=True)  16.2 us
    reduce_sum x56, other arithmetic, orthonormal(): jnp.sum(vec_real * vec_real + vec_imag * vec_imag, axis=-1, keepdims=True)  10.4 us
    all_to_all x1, blocking collectives, body(): return lax.all_to_all(scaled, 'tm', split_axis=1, concat_axis=0, tiled=True)  9.72 us
  transfers between devices with their start and end apart: 1, of which 1 were waited for; matrix products, arithmetic and copies ran while one was open for 2% of the time, Pallas kernels for 0%

profile of v1, /device:TPU:2, one launch (start us, length us, event | category | flops | bytes accessed | tf_op | source)
XLA Modules:
  0.0 419.9 jit_solution(15101036179375383621)
XLA Ops:
  1.1 1.2 constant_dynamic-update-slice_fusion.30
  16.7 3.2 copy-done.6
  19.9 6.2 %all-to-all-start = ((bf16[32,2,1,2,64,512]{5,4,3,2,1,0:T(8,128)(2,1)}), bf16[32,2,1,2,64,512]{5,4,3,2,1,0:T(8,128)(2,1)}, u32[]{:S(2)}, u32[]{:S(2)}) async-start(bf16[32,2,1,2,64,512]{5,4,3,2,1,0:T(8,128)(2,1)} %bitcast.1599), calls=%async_computation | async-start | bytes 16777216 | tf_op jit(solution)/shard_map/all_to_all | solution.py:77
  26.4 2.8 gather_fusion
  34.9 175.2 %all-to-all-done = bf16[32,2,1,2,64,512]{5,4,3,2,1,0:T(8,128)(2,1)} async-done(((bf16[32,2,1,2,64,512]{5,4,3,2,1,0:T(8,128)(2,1)}), bf16[32,2,1,2,64,512]{5,4,3,2,1,0:T(8,128)(2,1)}, u32[]{:S(2)}, u32[]{:S(2)}) %all-to-all-start) | async-done | bytes 8388640 | tf_op jit(solution)/shard_map/all_to_all | solution.py:77
  210.1 4.2 fusion.294
  240.3 1.6 fusion.65
  267.0 1.4 fusion.42
  291.0 118.1 %while.10 = (s32[]{:T(128)}, f32[2,1024]{1,0:T(2,128)S(1)}, bf16[2,2048,512]{2,1,0:T(8,128)(2,1)}, bf16[2,8,512]{2,0,1:T(2,128)(2,1)S(1)}, bf16[2,2048,512]{2,1,...) while((s32[]{:T(128)}, f32[2,1024]{1,0:T(2,128)S(1)}, ...), condition=%wide.region_450.451_spmd, body=%wide.region_448.0_spmd.sunk | while | flops 8755674112 | bytes 126480664 | solution.py:122
  315.0 2.2 fusion.463
  317.3 2.2 fusion.464
  319.5 2.4 fusion.460
  325.7 8.5 %fusion.470 = f32[2048,1024]{1,0:T(8,128)S(1)} fusion(bf16[2048,512]{1,0:T(8,128)(2,1)S(1)} %subtract_convert_fusion.4, f32[1024]{0:T(1024)S(1)} %bitcast.1637, f32[512]{0:T(512)S(1)} %bitcast.1645, f32[1024]{0:T(1024)S(1)} %bitcast.1633, f32[512]{0:T(512)S(1)} %bitcast.1641, f32[]{:T(128)} %bitcast.1547), kind=kOutput, calls=%fused_computation.23.clone.1 | convolution fusion | flops 2150105088 | bytes 10498052 | tf_op jit(solution)/shard_map/while/body/eval_jaxpr/dot_general | solution.py:35
  334.2 8.4 %fusion.467 = f32[2048,1024]{1,0:T(8,128)S(1)} fusion(bf16[2048,512]{1,0:T(8,128)(2,1)S(1)} %subtract_convert_fusion.4, f32[1024]{0:T(1024)S(1)} %bitcast.1638, f32[512]{0:T(512)S(1)} %bitcast.1646, f32[1024]{0:T(1024)S(1)} %bitcast.1634, f32[512]{0:T(512)S(1)} %bitcast.1642, f32[]{:T(128)} %bitcast.1547), kind=kOutput, calls=%fused_computation.21.clone.1 | convolution fusion | flops 2150105088 | bytes 10498052 | tf_op jit(solution)/shard_map/while/body/eval_jaxpr/dot_general | solution.py:35
  342.6 8.4 %fusion.469 = f32[2048,1024]{1,0:T(8,128)S(1)} fusion(bf16[2048,512]{1,0:T(8,128)(2,1)S(1)} %subtract_convert_fusion.5, f32[1024]{0:T(1024)S(1)} %bitcast.1639, f32[512]{0:T(512)S(1)} %bitcast.1647, f32[1024]{0:T(1024)S(1)} %bitcast.1635, f32[512]{0:T(512)S(1)} %bitcast.1643, f32[]{:T(128)} %bitcast.1547), kind=kOutput, calls=%fused_computation.22.clone.1 | convolution fusion | flops 2150105088 | bytes 10498052 | tf_op jit(solution)/shard_map/while/body/eval_jaxpr/dot_general | solution.py:35
  351.0 10.2 %add_reduce_fusion.198 = f32[1024]{0:T(1024)S(1)} fusion(f32[2048,1024]{1,0:T(8,128)S(1)} %fusion.467, f32[2048,1024]{1,0:T(8,128)S(1)} %fusion.469, f32[2048,1024]{1,0:T(8,128)S(1)} %fusion.470, bf16[2048,512]{1,0:T(8,128)(2,1)S(1)} %subtract_convert_fusion.5, f32[1024]{0:T(1024)S(1)} %bitcast.1640, f32[512]{0:T(512)S(1)} %bitcast.1648, ...), kind=kOutput, calls=%fused_computation.1.clone.1 | convolution fusion | flops 2162686976 | bytes 27279364 | tf_op jit(solution)/shard_map/while/body/eval_jaxpr/dot_general | solution.py:35
  362.8 2.2 fusion.463
  365.1 2.2 fusion.464
  367.3 2.4 fusion.460
  373.5 8.5 %fusion.470 = f32[2048,1024]{1,0:T(8,128)S(1)} fusion(bf16[2048,512]{1,0:T(8,128)(2,1)S(1)} %subtract_convert_fusion.4, f32[1024]{0:T(1024)S(1)} %bitcast.1637, f32[512]{0:T(512)S(1)} %bitcast.1645, f32[1024]{0:T(1024)S(1)} %bitcast.1633, f32[512]{0:T(512)S(1)} %bitcast.1641, f32[]{:T(128)} %bitcast.1547), kind=kOutput, calls=%fused_computation.23.clone.1 | convolution fusion | flops 2150105088 | bytes 10498052 | tf_op jit(solution)/shard_map/while/body/eval_jaxpr/dot_general | solution.py:35
  382.0 8.4 %fusion.467 = f32[2048,1024]{1,0:T(8,128)S(1)} fusion(bf16[2048,512]{1,0:T(8,128)(2,1)S(1)} %subtract_convert_fusion.4, f32[1024]{0:T(1024)S(1)} %bitcast.1638, f32[512]{0:T(512)S(1)} %bitcast.1646, f32[1024]{0:T(1024)S(1)} %bitcast.1634, f32[512]{0:T(512)S(1)} %bitcast.1642, f32[]{:T(128)} %bitcast.1547), kind=kOutput, calls=%fused_computation.21.clone.1 | convolution fusion | flops 2150105088 | bytes 10498052 | tf_op jit(solution)/shard_map/while/body/eval_jaxpr/dot_general | solution.py:35
  390.4 8.4 %fusion.469 = f32[2048,1024]{1,0:T(8,128)S(1)} fusion(bf16[2048,512]{1,0:T(8,128)(2,1)S(1)} %subtract_convert_fusion.5, f32[1024]{0:T(1024)S(1)} %bitcast.1639, f32[512]{0:T(512)S(1)} %bitcast.1647, f32[1024]{0:T(1024)S(1)} %bitcast.1635, f32[512]{0:T(512)S(1)} %bitcast.1643, f32[]{:T(128)} %bitcast.1547), kind=kOutput, calls=%fused_computation.22.clone.1 | convolution fusion | flops 2150105088 | bytes 10498052 | tf_op jit(solution)/shard_map/while/body/eval_jaxpr/dot_general | solution.py:35
  398.8 10.2 %add_reduce_fusion.198 = f32[1024]{0:T(1024)S(1)} fusion(f32[2048,1024]{1,0:T(8,128)S(1)} %fusion.467, f32[2048,1024]{1,0:T(8,128)S(1)} %fusion.469, f32[2048,1024]{1,0:T(8,128)S(1)} %fusion.470, bf16[2048,512]{1,0:T(8,128)(2,1)S(1)} %subtract_convert_fusion.5, f32[1024]{0:T(1024)S(1)} %bitcast.1640, f32[512]{0:T(512)S(1)} %bitcast.1648, ...), kind=kOutput, calls=%fused_computation.1.clone.1 | convolution fusion | flops 2162686976 | bytes 27279364 | tf_op jit(solution)/shard_map/while/body/eval_jaxpr/dot_general | solution.py:35
  409.1 9.7 %all_to_all.24 = f32[2,2,512]{2,0,1:T(2,128)S(1)} all-to-all(f32[2,2,512]{2,0,1:T(2,128)S(1)} %bitcast.1649), channel_id=1, replica_groups=mesh['chan'=16,'tm'=2] {'tm'}, dimensions={1} | all-to-all | bytes 16384 | tf_op jit(solution)/shard_map/all_to_all | solution.py:124
  (425 shorter events, 103.8 us)
Async XLA Ops:
  0.0 29.6 %copy-start = (s32[4,2]{0,1:T(2,128)S(1)}, s32[4,2]{0,1:T(2,128)}, u32[]{:S(2)}) copy-start(s32[4,2]{0,1:T(2,128)} %param.9) | copy-start | bytes 100
  0.0 16.2 %copy-start.7 = (bf16[2,64,64,512]{3,2,1,0:T(8,128)(2,1)S(1)}, bf16[2,64,64,512]{3,2,1,0:T(8,128)(2,1)}, u32[]{:S(2)}) copy-start(bf16[2,64,64,512]{3,2,1,0:T(8,128)(2,1)} %param.8) | copy-start | bytes 25165828
  16.7 3.2 copy-start.6
  19.9 6.2 %copy-start.11 = (f32[2,1024]{1,0:T(2,128)S(1)}, f32[2,1024]{1,0:T(2,128)}, u32[]{:S(2)}) copy-start(f32[2,1024]{1,0:T(2,128)} %param.12) | copy-start | bytes 24580
  19.9 6.5 %copy-start.10 = (s32[1024]{0:T(1024)S(1)}, s32[1024]{0:T(1024)}, u32[]{:S(2)}) copy-start(s32[1024]{0:T(1024)} %param.13) | copy-start | bytes 12292
  19.9 9.8 %copy-start.9 = (f32[2,4,8,512]{3,2,1,0:T(8,128)S(1)}, f32[2,4,8,512]{3,2,1,0:T(8,128)}, u32[]{:S(2)}) copy-start(f32[2,4,8,512]{3,2,1,0:T(8,128)} %param.10) | copy-start | bytes 393220
  19.9 190.2 %all-to-all-start = ((bf16[32,2,1,2,64,512]{5,4,3,2,1,0:T(8,128)(2,1)}), bf16[32,2,1,2,64,512]{5,4,3,2,1,0:T(8,128)(2,1)}, u32[]{:S(2)}, u32[]{:S(2)}) async-start(bf16[32,2,1,2,64,512]{5,4,3,2,1,0:T(8,128)(2,1)} %bitcast.1599), calls=%async_computation | async-start | bytes 16777216 | tf_op jit(solution)/shard_map/all_to_all | solution.py:77
  214.8 69.8 %copy-start.2 = (bf16[1,1,2,32,64,512]{5,4,3,2,1,0:T(8,128)(2,1)}, bf16[1,1,2,32,64,512]{5,4,3,2,1,0:T(8,128)(2,1)S(1)}, u32[]{:S(2)}) copy-start(bf16[1,1,2,32,64,512]{5,4,3,2,1,0:T(8,128)(2,1)S(1)} %copy.2265) | copy-start | bytes 12582916
  215.3 69.9 %copy-start.4 = (bf16[1,1,2,32,64,512]{5,4,3,2,1,0:T(8,128)(2,1)}, bf16[1,1,2,32,64,512]{5,4,3,2,1,0:T(8,128)(2,1)S(1)}, u32[]{:S(2)}) copy-start(bf16[1,1,2,32,64,512]{5,4,3,2,1,0:T(8,128)(2,1)S(1)} %copy.2262) | copy-start | bytes 12582916
  284.6 6.4 %copy-start.8 = (f32[2,512]{1,0:T(2,128)S(1)}, f32[2,512]{1,0:T(2,128)}, u32[]{:S(2)}) copy-start(f32[2,512]{1,0:T(2,128)} %param.11) | copy-start | bytes 12292
  313.5 8.4 %copy-start.3 = (bf16[2,2048,512]{2,1,0:T(8,128)(2,1)S(1)}, bf16[2,2048,512]{2,1,0:T(8,128)(2,1)}, u32[]{:S(2)}) copy-start(bf16[2,2048,512]{2,1,0:T(8,128)(2,1)} %get-tuple-element.1442) | copy-start | bytes 12582916 | tf_op jit(solution)/shard_map/while
  319.5 3.8 copy-start.5
  361.3 8.4 %copy-start.3 = (bf16[2,2048,512]{2,1,0:T(8,128)(2,1)S(1)}, bf16[2,2048,512]{2,1,0:T(8,128)(2,1)}, u32[]{:S(2)}) copy-start(bf16[2,2048,512]{2,1,0:T(8,128)(2,1)} %get-tuple-element.1442) | copy-start | bytes 12582916 | tf_op jit(solution)/shard_map/while
  367.3 3.8 copy-start.5
  409.1 10.4 %copy-start.1 = (s32[4,2]{0,1:T(2,128)S(1)}, s32[4,2]{0,1:T(2,128)}, u32[]{:S(2)}) copy-start(s32[4,2]{0,1:T(2,128)} %param.9) | copy-start | bytes 100
